TPU v7x, 32 devices: a whole 2x2x4 slice. The times are simulated.
32 devices in a mesh: row: 8 (over z, core), col: 4 (over y, x).
Axes of the slice: x: 2, y: 2, z: 4, core: 2. Of those that a mesh axis runs over, the one named last changes fastest.
Arguments:
- diag_tile: float32 [128, 128], P('row'), may hold values from -20 to 100, as said below
- panel: bfloat16 [16384, 128], P(('row', 'col')), may hold values from -1.796875 to 1.796875
- trailing: float32 [16384, 2048], P('row', 'col'), may hold values from -6 to 6
Outputs:
- solved: bfloat16 [16384, 128], P(('row', 'col'))
- updated: float32 [16384, 2048], P('row', 'col')
Inputs may be any that keep to these rules, and one draw needn't show every extreme that they name: diag_tile is symmetric and positive definite, with its smallest eigenvalue 1 or more.
All inputs are finite; a program needn't handle non-finite values.
Results may differ from a plain program's by a relative error of at most 0.0051.
Values may be sent and summed in bfloat16 or wider, within the bound.
No kernel may reach another device: no remote copies, remote signals or barrier semaphores. Data moves between devices by JAX's collectives and lax.ppermute only.
A program may use at most 64 MiB of HBM per device.

v0:
```python
import jax
import jax.numpy as jnp
from jax import lax
from jax.sharding import PartitionSpec as P


def from_root(value, axis, source):
    kept = jnp.where(lax.axis_index(axis) == source, value, 0).astype(value.dtype)
    return lax.psum(kept, axis)


def per_device(diag_tile, panel, trailing):
    whole_tile = lax.all_gather(diag_tile, "row", axis=0, tiled=True)
    factor = jnp.linalg.cholesky(whole_tile)
    identity = jnp.eye(whole_tile.shape[0], dtype=whole_tile.dtype)
    inverse = lax.linalg.triangular_solve(factor, identity, left_side=True, lower=True).astype(
        jnp.bfloat16
    )
    solved_rows = lax.dot_general(
        panel, inverse, (((1,), (1,)), ((), ())), preferred_element_type=jnp.float32
    ).astype(jnp.bfloat16)
    row_panel = lax.all_gather(solved_rows, "col", axis=0, tiled=True)
    rows_dev = row_panel.shape[0]
    cols_dev = trailing.shape[1]
    col_start = lax.axis_index("col") * cols_dev
    source_row = col_start // rows_dev
    offset = col_start % rows_dev
    picked = lax.dynamic_slice_in_dim(row_panel, offset, cols_dev, 0)
    col_panel = from_root(picked, "row", source_row)
    update = lax.dot_general(
        row_panel, col_panel, (((1,), (1,)), ((), ())), preferred_element_type=jnp.float32
    )
    row_ids = lax.axis_index("row") * rows_dev + jnp.arange(rows_dev, dtype=jnp.int32)
    col_ids = col_start + jnp.arange(cols_dev, dtype=jnp.int32)
    lower_part = row_ids[:, None] >= col_ids[None, :]
    updated = jnp.where(lower_part, trailing - update, trailing)
    return (solved_rows, updated)


def solution(mesh):
    in_specs = (P("row", None), P(("row", "col"), None), P("row", "col"))
    out_specs = (P(("row", "col"), None), P("row", "col"))
    return jax.shard_map(
        per_device, mesh=mesh, in_specs=in_specs, out_specs=out_specs, check_vma=False
    )
```

profile of v0, /device:TPU:0, one launch (start us, length us, event | category | flops | bytes accessed | tf_op | source)
XLA Modules:
  0.0 123.7 jit_solution(9039450617726350077)
XLA Ops:
  7.2 0.0 copy-start
  7.2 0.0 all-reduce.2.cloned.1.call-start
  7.2 15.9 %all_gather.6 = f32[128,128]{1,0:T(8,128)S(1)} all-gather(f32[16,128]{1,0:T(8,128)} %param.3), channel_id=1, replica_groups=mesh['row'=8,'col'=4] {'row'}, dimensions={0}, use_global_device_ids=true | all-gather | bytes 73728 | tf_op jit(solution)/shard_map/all_gather | solution.py:13
  23.2 0.1 copy.8
  23.3 11.7 %cholesky.17 = f32[128,128]{1,0:T(8,128)S(1)} custom-call(f32[128,128]{1,0:T(8,128)S(1)} %fusion.3), custom_call_target="Cholesky" | custom-call | tf_op jit(solution)/shard_map/jit(cholesky)/cholesky | solution.py:14
  35.0 0.6 compare_reduce_fusion
  35.7 0.7 fusion.1
  36.3 9.8 %custom-call.6 = f32[1,128,128]{1,2,0:T(8,128)S(1)} custom-call(f32[1,128,128]{2,1,0:T(8,128)S(1)} %fusion.1), custom_call_target="InvertDiagBlocksLowerTriangular" | custom-call | tf_op jit(solution)/shard_map/triangular_solve | solution.py:16
  46.1 0.3 convolution_convert_fusion.1
  46.4 0.0 copy-done
  46.4 0.2 fusion
  46.6 10.3 %all_gather.7 = bf16[2048,128]{0,1:T(8,128)(2,1)S(1)} all-gather(bf16[512,128]{0,1:T(8,128)(2,1)S(1)} %fusion), channel_id=1, replica_groups=mesh['row'=8,'col'=4] {'col'}, dimensions={0}, use_global_device_ids=true | all-gather | bytes 655360 | tf_op jit(solution)/shard_map/all_gather | solution.py:22
  56.9 0.7 dynamic-slice_select_fusion
  57.6 0.0 all-reduce.2.cloned.1.call-update
  57.6 0.8 copy.9
  58.4 54.4 %all-reduce.2.cloned.1.call-done = bf16[512,128]{0,1:T(8,128)(2,1)} async-done(((bf16[512,128]{0,1:T(8,128)(2,1)}), bf16[512,128]{0,1:T(8,128)(2,1)}) %all-reduce.2.cloned.1.call-update) | async-done | bytes 131088 | tf_op jit(solution)/shard_map/psum | solution.py:9
  112.8 4.1 %subtract_select_fusion = f32[2048,512]{1,0:T(8,128)} fusion(f32[2048,512]{1,0:T(8,128)} %param.5, bf16[2048,128]{0,1:T(8,128)(2,1)S(1)} %all_gather.7, bf16[512,128]{0,1:T(8,128)(2,1)} %all-reduce.2.cloned.1.call-done, s32[512]{0:T(512)S(1)} %iota_add_fusion.1, s32[2048]{0:T(1024)S(1)} %iota_add_fusion), kind=kOutput, calls=%fused_computation | convolution fusion | flops 271581184 | bytes 9054208 | tf_op jit(solution)/shard_map/dot_general | solution.py:30
  (4 shorter events, 0.1 us)
Async XLA Ops:
  7.2 39.2 %copy-start = (bf16[512,128]{1,0:T(8,128)(2,1)S(1)}, bf16[512,128]{1,0:T(8,128)(2,1)}, u32[]{:S(2)}) copy-start(bf16[512,128]{1,0:T(8,128)(2,1)} %param.4) | copy-start | bytes 393220
  7.2 105.6 %all-reduce.2.cloned.1.call-start = ((), (), s32[]{:S(2)}) async-start(), calls=%async_computation | async-start | bytes 262144 | tf_op jit(solution)/shard_map/psum | solution.py:9
Sparse Core Ops, SparseCore 0:
  57.7 55.0 all-reduce.1
where the time goes:
time: 124 us
  waiting for transfers between devices  54.4 us (44%)
  blocking collectives  26.2 us (21%)
  other arithmetic  23.6 us (19%)
  between operations  14.1 us (11%)
  matrix products  4.52 us (4%)
    psum x1, waiting for transfers between devices, from_root(): return lax.psum(kept, axis)  54.4 us
    all_gather x1, blocking collectives, per_device(): whole_tile = lax.all_gather(diag_tile, 'row', axis=0, tiled=True)  15.9 us
    another operation x3, other arithmetic, per_device(): factor = jnp.linalg.cholesky(whole_tile)  12.4 us
    another operation x2, other arithmetic, per_device(): lax.linalg.triangular_solve(factor, identity, left_side=True, lower=True)  10.5 us
    all_gather x1, blocking collectives, per_device(): row_panel = lax.all_gather(solved_rows, 'col', axis=0, tiled=True)  10.3 us
    dot_general x1, matrix products, per_device(): lax.dot_general(row_panel, col_panel, (((1,), (1,)), ((), ())), preferred...  4.08 us
  transfers between devices with their start and end apart: 1, of which 1 were waited for; matrix products, arithmetic and copies ran while one was open for 1% of the time, Pallas kernels for 0%

commit v1 on v0

--- a/solution.py
+++ b/solution.py
@@ -6,7 +6,7 @@
 
 def from_root(value, axis, source):
     kept = jnp.where(lax.axis_index(axis) == source, value, 0).astype(value.dtype)
-    return lax.psum(kept, axis)
+    return jnp.sum(lax.all_gather(kept, axis), axis=0)
 
 
 def per_device(diag_tile, panel, trailing):

time: 124 us -> 93.6 us (0.75)
  waiting for transfers between devices: 54.4 us -> 21.7 us
  local copies, waits for them, and re-layouts: 0.86 us -> 2.48 us
    psum x1 -> x0, waiting for transfers between devices: 54.4 us -> none  [from_root(): return lax.psum(kept, axis)]
    all_gather x0 -> x1, waiting for transfers between devices: none -> 21.7 us  [from_root(): return jnp.sum(lax.all_gather(kept, axis), axis=0)]
    unnamed x3 -> x4, local copies, waits for them, and re-layouts: 0.77 us -> 2.39 us
where the time goes in v1:
time: 93.6 us; the launch traced here: 93.4 us
  blocking collectives  26.2 us (28%)
  other arithmetic  24.3 us (26%)
  waiting for transfers between devices  21.7 us (23%)
  between operations  14.1 us (15%)
  matrix products  4.53 us (5%)
  local copies, waits for them, and re-layouts  2.48 us (3%)
    all_gather x1, waiting for transfers between devices, from_root(): return jnp.sum(lax.all_gather(kept, axis), axis=0)  21.7 us
    all_gather x1, blocking collectives, per_device(): whole_tile = lax.all_gather(diag_tile, 'row', axis=0, tiled=True)  15.9 us
    another operation x3, other arithmetic, per_device(): factor = jnp.linalg.cholesky(whole_tile)  12.4 us
    another operation x2, other arithmetic, per_device(): lax.linalg.triangular_solve(factor, identity, left_side=True, lower=True)  10.5 us
    all_gather x1, blocking collectives, per_device(): row_panel = lax.all_gather(solved_rows, 'col', axis=0, tiled=True)  10.3 us
    dot_general x1, matrix products, per_device(): lax.dot_general(row_panel, col_panel, (((1,), (1,)), ((), ())), preferred...  4.08 us
    unnamed x4, local copies, waits for them, and re-layouts  2.39 us
  transfers between devices with their start and end apart: 1, of which 1 were waited for; matrix products, arithmetic and copies ran while one was open for 1% of the time, Pallas kernels for 0%

profile of v1, /device:TPU:0, one launch (start us, length us, event | category | flops | bytes accessed | tf_op | source)
XLA Modules:
  0.0 93.4 jit_solution(12331205428901651391)
XLA Ops:
  7.2 0.0 copy-start
  7.2 0.0 all-gather.3.cloned.1.call-start
  7.2 15.9 %all_gather.12 = f32[128,128]{1,0:T(8,128)S(1)} all-gather(f32[16,128]{1,0:T(8,128)} %param.3), channel_id=1, replica_groups=mesh['row'=8,'col'=4] {'row'}, dimensions={0}, use_global_device_ids=true | all-gather | bytes 73728 | tf_op jit(solution)/shard_map/all_gather | solution.py:13
  23.2 0.1 copy.8
  23.3 11.7 %cholesky.17 = f32[128,128]{1,0:T(8,128)S(1)} custom-call(f32[128,128]{1,0:T(8,128)S(1)} %fusion.3), custom_call_target="Cholesky" | custom-call | tf_op jit(solution)/shard_map/jit(cholesky)/cholesky | solution.py:14
  35.0 0.6 compare_reduce_fusion
  35.7 0.7 fusion.1
  36.3 9.8 %custom-call.6 = f32[1,128,128]{1,2,0:T(8,128)S(1)} custom-call(f32[1,128,128]{2,1,0:T(8,128)S(1)} %fusion.1), custom_call_target="InvertDiagBlocksLowerTriangular" | custom-call | tf_op jit(solution)/shard_map/triangular_solve | solution.py:16
  46.1 0.3 convolution_convert_fusion.1
  46.4 0.0 copy-done
  46.4 0.2 fusion
  46.6 10.3 %all_gather.13 = bf16[2048,128]{0,1:T(8,128)(2,1)S(1)} all-gather(bf16[512,128]{0,1:T(8,128)(2,1)S(1)} %fusion), channel_id=1, replica_groups=mesh['row'=8,'col'=4] {'col'}, dimensions={0}, use_global_device_ids=true | all-gather | bytes 655360 | tf_op jit(solution)/shard_map/all_gather | solution.py:22
  56.9 0.7 dynamic-slice_select_fusion
  57.6 0.0 all-gather.3.cloned.1.call-update
  57.6 0.8 copy.9
  58.4 21.7 %all-gather.3.cloned.1.call-done = bf16[4096,128]{0,1:T(8,128)(2,1)} async-done(((bf16[512,128]{0,1:T(8,128)(2,1)}), bf16[4096,128]{0,1:T(8,128)(2,1)}) %all-gather.3.cloned.1.call-update) | async-done | bytes 1048592 | tf_op jit(solution)/shard_map/all_gather | solution.py:9
  80.1 1.6 %copy.10 = bf16[16,8,8,512]{3,2,1,0:T(8,128)(2,1)S(1)} copy(bf16[16,8,8,512]{3,1,2,0:T(8,128)(2,1)} %bitcast.20) | data formatting | bytes 2097152
  81.7 0.8 bitcast_reduce_fusion
  82.5 4.1 %subtract_select_fusion = f32[2048,512]{1,0:T(8,128)} fusion(f32[2048,512]{1,0:T(8,128)} %param.5, bf16[2048,128]{0,1:T(8,128)(2,1)S(1)} %all_gather.13, bf16[512,128]{0,1:T(8,128)(2,1)S(1)} %bitcast_reduce_fusion, s32[512]{0:T(512)S(1)} %iota_add_fusion.1, s32[2048]{0:T(1024)S(1)} %iota_add_fusion), kind=kOutput, calls=%fused_computation | convolution fusion | flops 271581184 | bytes 9054208 | tf_op jit(solution)/shard_map/dot_general | solution.py:30
  (4 shorter events, 0.1 us)
Async XLA Ops:
  7.2 39.2 %copy-start = (bf16[512,128]{1,0:T(8,128)(2,1)S(1)}, bf16[512,128]{1,0:T(8,128)(2,1)}, u32[]{:S(2)}) copy-start(bf16[512,128]{1,0:T(8,128)(2,1)} %param.4) | copy-start | bytes 393220
  7.2 72.9 %all-gather.3.cloned.1.call-start = ((), (), s32[]{:S(2)}) async-start(), calls=%async_computation | async-start | bytes 1179648 | tf_op jit(solution)/shard_map/all_gather | solution.py:9
Sparse Core Ops, SparseCore 0:
  57.7 22.2 all-gather.2
